TPU v7x, 32 devices: a whole 2x2x4 slice. The times are simulated.
32 devices in a mesh: dp: 8 (over y, x, core), mp: 4 (over z).
Axes of the slice: x: 2, y: 2, z: 4, core: 2. Of those that a mesh axis runs over, the one named last changes fastest.
Arguments:
- tokens: bfloat16 [12288, 1792], P(('dp', 'mp')), may hold values from -6 to 6
- cotangent: bfloat16 [12288, 1792], P(('dp', 'mp')), may hold values from -6 to 6
- route: int32 [12288], P(('dp', 'mp')), may hold values from 0 to 12287, as said below
- lengths: int32 [8, 3], P('dp'), may hold values from 1 to 1024, 1536 in all within a row
- key_mask: int32 [12288], P('dp'), may hold values 0 or 1
- norm1_gain: float32 [1792], replicated, may hold values from 0.1 to 1.9
- norm2_gain: float32 [1792], replicated, may hold values from 0.1 to 1.9
- w_query: bfloat16 [1792, 1792], P(None, 'mp'), may hold values from -0.1875 to 0.1875
- w_key: bfloat16 [1792, 1792], P(None, 'mp'), may hold values from -0.1875 to 0.1875
- w_value: bfloat16 [1792, 1792], P(None, 'mp'), may hold values from -0.125 to 0.125
- w_out: bfloat16 [1792, 1792], P('mp'), may hold values from -0.375 to 0.375
- w_gate: bfloat16 [1792, 4096], P(None, 'mp'), may hold values from -0.125 to 0.125
- w_up: bfloat16 [1792, 4096], P(None, 'mp'), may hold values from -0.125 to 0.125
- w_down: bfloat16 [4096, 1792], P('mp'), may hold values from -0.125 to 0.125
Outputs:
- output: bfloat16 [12288, 1792], P(('dp', 'mp'))
- input_grad: bfloat16 [12288, 1792], P(('dp', 'mp'))
- norm1_gain_grad: float32 [1792], replicated
- norm2_gain_grad: float32 [1792], replicated
- w_query_grad: float32 [1792, 1792], P(None, 'mp')
- w_key_grad: float32 [1792, 1792], P(None, 'mp')
- w_value_grad: float32 [1792, 1792], P(None, 'mp')
- w_out_grad: float32 [1792, 1792], P('mp')
- w_gate_grad: float32 [1792, 4096], P(None, 'mp')
- w_up_grad: float32 [1792, 4096], P(None, 'mp')
- w_down_grad: float32 [4096, 1792], P('mp')
Inputs may be any that keep to these rules, and one draw needn't show every extreme that they name: route is a permutation of the 12288 slots. For every row r, slot s = route[r] lies on index s // 1536 of dp and on index (s // 384) % (number of mp indices) of mp, and that mp index equals the mp index of the device that holds row r in given order; every device holds exactly 48 rows bound for each index of dp. Each row of lengths sums to 1536; its largest entry is exactly 1024.
All inputs are finite; a program needn't handle non-finite values. No bound on the sum of `key_mask` on one device may be relied on, other than what follows from the above.
Results may differ from a plain program's by a relative error of at most 0.019.
Values may be sent and summed in bfloat16 or wider, within the bound.
A program may use at most 192 MiB of HBM per device.

v0:
```python
import jax
import jax.numpy as jnp
from jax import lax
from jax.sharding import PartitionSpec as P

HEAD_DIM = 112
WINDOW = 64
TOK_DEV = 1536
EPSILON = 1e-05
MASKED = 1e30


def norm_rows(values):
    inverse = lax.rsqrt(jnp.mean(values * values, axis=-1, keepdims=True) + EPSILON)
    return (values * inverse, inverse)


def norm_back(gradient, normed, inverse, norm_gain):
    scaled = gradient * norm_gain
    result = inverse * (scaled - normed * jnp.mean(scaled * normed, axis=-1, keepdims=True))
    return (result, jnp.sum(gradient * normed, axis=0))


def padded(values, filler):
    front = jnp.full((WINDOW,) + values.shape[1:], filler, values.dtype)
    return jnp.concatenate([front, values], axis=0)


def block_scores(query_block, key_block, query_seg, key_seg, key_flag, first_row, score_scale):
    query_pos = first_row + jnp.arange(query_block.shape[0], dtype=jnp.int32)
    key_pos = first_row - WINDOW + jnp.arange(key_block.shape[0], dtype=jnp.int32)
    distance = query_pos[:, None] - key_pos[None, :]
    allowed = (distance >= 0) & (distance < WINDOW) & (query_seg[:, None] == key_seg[None, :])
    allowed = allowed & ((key_flag[None, :] == 1) | (distance == 0))
    raw_scores = (
        jnp.einsum("qhd,khd->hqk", query_block, key_block, preferred_element_type=jnp.float32)
        * score_scale
    )
    return jnp.where(allowed[None], raw_scores, -MASKED)


def block_inputs(query, key_pad, value_pad, segment, seg_pad, live_pad, first_row, block_rows):
    key_span = block_rows + WINDOW
    return (
        lax.dynamic_slice_in_dim(query, first_row, block_rows, 0),
        lax.dynamic_slice_in_dim(key_pad, first_row, key_span, 0),
        lax.dynamic_slice_in_dim(value_pad, first_row, key_span, 0),
        lax.dynamic_slice_in_dim(segment, first_row, block_rows, 0),
        lax.dynamic_slice_in_dim(seg_pad, first_row, key_span, 0),
        lax.dynamic_slice_in_dim(live_pad, first_row, key_span, 0),
    )


def attend_forward(query, key_all, value_all, segment, key_live):
    token_count, head_count, head_width = query.shape
    block_rows = min(512, token_count)
    score_scale = head_width ** (-0.5)
    key_pad = padded(key_all, 0.0)
    value_pad = padded(value_all, 0.0)
    seg_pad = padded(segment, -1)
    live_pad = padded(key_live, 0)

    def one_block(running, block_index):
        first_row = block_index * block_rows
        query_block, key_block, value_block, query_seg, key_seg, key_flag = block_inputs(
            query, key_pad, value_pad, segment, seg_pad, live_pad, first_row, block_rows
        )
        scores = block_scores(
            query_block, key_block, query_seg, key_seg, key_flag, first_row, score_scale
        )
        row_max = jnp.max(scores, axis=-1, keepdims=True)
        weights = jnp.exp(scores - row_max)
        denominator = jnp.sum(weights, axis=-1, keepdims=True)
        chances = (weights / denominator).astype(jnp.bfloat16)
        mixed = jnp.einsum("hqk,khd->qhd", chances, value_block, preferred_element_type=jnp.float32)
        return (
            running,
            (mixed.astype(jnp.bfloat16), row_max[..., 0] + jnp.log(denominator[..., 0])),
        )

    _, (mixed, logsum) = lax.scan(
        one_block, jnp.zeros((), jnp.int32), jnp.arange(token_count // block_rows, dtype=jnp.int32)
    )
    return (mixed.reshape(token_count, head_count * head_width), logsum)


def attend_backward(query, key_all, value_all, segment, key_live, logsum, mixed_grad):
    token_count, head_count, head_width = query.shape
    block_rows = min(512, token_count)
    key_span = block_rows + WINDOW
    score_scale = head_width ** (-0.5)
    key_pad = padded(key_all, 0.0)
    value_pad = padded(value_all, 0.0)
    seg_pad = padded(segment, -1)
    live_pad = padded(key_live, 0)

    def one_block(running, inputs):
        key_grad, value_grad = running
        block_index, block_logsum = inputs
        first_row = block_index * block_rows
        query_block, key_block, value_block, query_seg, key_seg, key_flag = block_inputs(
            query, key_pad, value_pad, segment, seg_pad, live_pad, first_row, block_rows
        )
        grad_block = lax.dynamic_slice_in_dim(mixed_grad, first_row, block_rows, 0)
        scores = block_scores(
            query_block, key_block, query_seg, key_seg, key_flag, first_row, score_scale
        )
        chances = jnp.exp(scores - block_logsum[..., None])
        chance_grad = jnp.einsum(
            "qhd,khd->hqk", grad_block, value_block, preferred_element_type=jnp.float32
        )
        row_dot = jnp.sum(chances * chance_grad, axis=-1, keepdims=True)
        score_grad = (chances * (chance_grad - row_dot)).astype(jnp.bfloat16)
        query_grad = (
            jnp.einsum("hqk,khd->qhd", score_grad, key_block, preferred_element_type=jnp.float32)
            * score_scale
        )
        key_part = (
            jnp.einsum("hqk,qhd->khd", score_grad, query_block, preferred_element_type=jnp.float32)
            * score_scale
        )
        value_part = jnp.einsum(
            "hqk,qhd->khd",
            chances.astype(jnp.bfloat16),
            grad_block,
            preferred_element_type=jnp.float32,
        )
        key_grad = lax.dynamic_update_slice_in_dim(
            key_grad,
            lax.dynamic_slice_in_dim(key_grad, first_row, key_span, 0) + key_part,
            first_row,
            0,
        )
        value_grad = lax.dynamic_update_slice_in_dim(
            value_grad,
            lax.dynamic_slice_in_dim(value_grad, first_row, key_span, 0) + value_part,
            first_row,
            0,
        )
        return ((key_grad, value_grad), query_grad)

    empty_grad = jnp.zeros((token_count + WINDOW, head_count, head_width), jnp.float32)
    (key_grad, value_grad), query_grad = lax.scan(
        one_block,
        (empty_grad, empty_grad),
        (jnp.arange(token_count // block_rows, dtype=jnp.int32), logsum),
    )
    flat_width = head_count * head_width
    return (
        query_grad.reshape(token_count, flat_width).astype(jnp.bfloat16),
        key_grad[WINDOW:].reshape(token_count, flat_width).astype(jnp.bfloat16),
        value_grad[WINDOW:].reshape(token_count, flat_width).astype(jnp.bfloat16),
    )


def local(
    tokens,
    cotangent,
    route,
    lengths,
    key_mask,
    norm1_gain,
    norm2_gain,
    w_query,
    w_key,
    w_value,
    w_out,
    w_gate,
    w_up,
    w_down,
):
    groups = lax.axis_size("dp")
    members = lax.axis_size("mp")
    member = lax.axis_index("mp")
    local_rows = tokens.shape[0]
    group_rows = local_rows * members
    bucket = local_rows // groups
    target = route // TOK_DEV
    chosen = (target[:, None] == jnp.arange(groups, dtype=jnp.int32)[None, :]).astype(jnp.int32)
    ranking = jnp.sum((jnp.cumsum(chosen, axis=0) - chosen) * chosen, axis=1)
    send_at = target * bucket + ranking
    arrival, arrival_grad, arrival_slot = (
        lax.all_to_all(
            jnp.zeros_like(tokens).at[send_at].set(tokens),
            "dp",
            split_axis=0,
            concat_axis=0,
            tiled=True,
        ),
        lax.all_to_all(
            jnp.zeros_like(cotangent).at[send_at].set(cotangent),
            "dp",
            split_axis=0,
            concat_axis=0,
            tiled=True,
        ),
        lax.all_to_all(
            jnp.zeros_like(route).at[send_at].set(route % local_rows),
            "dp",
            split_axis=0,
            concat_axis=0,
            tiled=True,
        ),
    )
    token_rows = jnp.zeros_like(arrival).at[arrival_slot].set(arrival)
    grad_rows = jnp.zeros_like(arrival_grad).at[arrival_slot].set(arrival_grad)
    seq_ends = jnp.cumsum(lengths[0])
    positions = jnp.arange(group_rows, dtype=jnp.int32)
    segment = jnp.sum((positions[:, None] >= seq_ends[None, :]).astype(jnp.int32), axis=1)
    input_rows = token_rows.astype(jnp.float32)
    normed_one, inverse_one = norm_rows(input_rows)
    leading_all, grad_all = (
        lax.all_gather(token_rows, "mp", axis=0, tiled=True),
        lax.all_gather(grad_rows, "mp", axis=0, tiled=True),
    )
    input_all = leading_all.astype(jnp.float32)
    normed_all, _ = norm_rows(input_all)
    hidden_one = (normed_all * norm1_gain).astype(jnp.bfloat16)
    head_count = w_query.shape[1] // HEAD_DIM
    query = jnp.dot(hidden_one, w_query, preferred_element_type=jnp.float32).astype(jnp.bfloat16)
    keys = jnp.dot(hidden_one, w_key, preferred_element_type=jnp.float32).astype(jnp.bfloat16)
    values = jnp.dot(hidden_one, w_value, preferred_element_type=jnp.float32).astype(jnp.bfloat16)
    query_heads = query.reshape(group_rows, head_count, HEAD_DIM)
    key_heads = keys.reshape(group_rows, head_count, HEAD_DIM)
    value_heads = values.reshape(group_rows, head_count, HEAD_DIM)
    mixed_flat, logsum = attend_forward(query_heads, key_heads, value_heads, segment, key_mask)
    attention_all = lax.psum(jnp.dot(mixed_flat, w_out, preferred_element_type=jnp.float32), "mp")
    middle_all = input_all + attention_all
    middle_rows = lax.dynamic_slice_in_dim(middle_all, member * local_rows, local_rows, 0)
    normed_mid, _ = norm_rows(middle_all)
    hidden_two = (normed_mid * norm2_gain).astype(jnp.bfloat16)
    normed_two, inverse_two = norm_rows(middle_rows)
    gate_value = jnp.dot(hidden_two, w_gate, preferred_element_type=jnp.float32)
    upward = jnp.dot(hidden_two, w_up, preferred_element_type=jnp.float32)
    sigmoid = jax.nn.sigmoid(gate_value)
    activated = (gate_value * sigmoid * upward).astype(jnp.bfloat16)
    out_rows = middle_rows + lax.psum_scatter(
        jnp.dot(activated, w_down, preferred_element_type=jnp.float32).astype(jnp.bfloat16),
        "mp",
        scatter_dimension=0,
        tiled=True,
    ).astype(jnp.float32)
    activated_grad = jnp.einsum("td,fd->tf", grad_all, w_down, preferred_element_type=jnp.float32)
    gate_grad = (activated_grad * upward * sigmoid * (1.0 + gate_value * (1.0 - sigmoid))).astype(
        jnp.bfloat16
    )
    upward_grad = (activated_grad * gate_value * sigmoid).astype(jnp.bfloat16)
    down_sum = jnp.einsum("tf,td->fd", activated, grad_all, preferred_element_type=jnp.float32)
    gate_sum = jnp.einsum("td,tf->df", hidden_two, gate_grad, preferred_element_type=jnp.float32)
    upward_sum = jnp.einsum(
        "td,tf->df", hidden_two, upward_grad, preferred_element_type=jnp.float32
    )
    hidden_two_grad = lax.psum_scatter(
        jnp.einsum("tf,df->td", gate_grad, w_gate, preferred_element_type=jnp.float32)
        + jnp.einsum("tf,df->td", upward_grad, w_up, preferred_element_type=jnp.float32),
        "mp",
        scatter_dimension=0,
        tiled=True,
    )
    norm_part_two, gain_two_grad = norm_back(hidden_two_grad, normed_two, inverse_two, norm2_gain)
    middle_grad = grad_rows.astype(jnp.float32) + norm_part_two
    branch_all = lax.all_gather(middle_grad.astype(jnp.bfloat16), "mp", axis=0, tiled=True)
    output_sum = jnp.einsum("tc,td->cd", mixed_flat, branch_all, preferred_element_type=jnp.float32)
    mixed_grad = jnp.einsum(
        "td,cd->tc", branch_all, w_out, preferred_element_type=jnp.float32
    ).astype(jnp.bfloat16)
    query_grad, key_grad, value_grad = attend_backward(
        query_heads,
        key_heads,
        value_heads,
        segment,
        key_mask,
        logsum,
        mixed_grad.reshape(group_rows, head_count, HEAD_DIM),
    )
    query_sum = jnp.einsum("td,tc->dc", hidden_one, query_grad, preferred_element_type=jnp.float32)
    key_sum = jnp.einsum("td,tc->dc", hidden_one, key_grad, preferred_element_type=jnp.float32)
    value_sum = jnp.einsum("td,tc->dc", hidden_one, value_grad, preferred_element_type=jnp.float32)
    hidden_one_grad = lax.psum_scatter(
        (
            jnp.einsum("tc,dc->td", query_grad, w_query, preferred_element_type=jnp.float32)
            + jnp.einsum("tc,dc->td", key_grad, w_key, preferred_element_type=jnp.float32)
            + jnp.einsum("tc,dc->td", value_grad, w_value, preferred_element_type=jnp.float32)
        ).astype(jnp.bfloat16),
        "mp",
        scatter_dimension=0,
        tiled=True,
    ).astype(jnp.float32)
    norm_part_one, gain_one_grad = norm_back(hidden_one_grad, normed_one, inverse_one, norm1_gain)
    input_grad = middle_grad + norm_part_one
    gain_one_sum, gain_two_sum = lax.psum((gain_one_grad, gain_two_grad), ("dp", "mp"))
    weight_sums = (
        lax.psum(query_sum.astype(jnp.bfloat16), "dp").astype(jnp.float32),
        lax.psum(key_sum.astype(jnp.bfloat16), "dp").astype(jnp.float32),
        lax.psum(value_sum.astype(jnp.bfloat16), "dp").astype(jnp.float32),
        lax.psum(output_sum.astype(jnp.bfloat16), "dp").astype(jnp.float32),
        lax.psum(gate_sum.astype(jnp.bfloat16), "dp").astype(jnp.float32),
        lax.psum(upward_sum.astype(jnp.bfloat16), "dp").astype(jnp.float32),
        lax.psum(down_sum.astype(jnp.bfloat16), "dp").astype(jnp.float32),
    )
    back_out, back_grad = (
        lax.all_to_all(
            out_rows.astype(jnp.bfloat16)[arrival_slot],
            "dp",
            split_axis=0,
            concat_axis=0,
            tiled=True,
        ),
        lax.all_to_all(
            input_grad.astype(jnp.bfloat16)[arrival_slot],
            "dp",
            split_axis=0,
            concat_axis=0,
            tiled=True,
        ),
    )
    return (
        back_out[send_at],
        back_grad[send_at],
        gain_one_sum,
        gain_two_sum,
        weight_sums[0],
        weight_sums[1],
        weight_sums[2],
        weight_sums[3],
        weight_sums[4],
        weight_sums[5],
        weight_sums[6],
    )


def solution(mesh):
    in_specs = (
        P(("dp", "mp"), None),
        P(("dp", "mp"), None),
        P(("dp", "mp")),
        P("dp", None),
        P("dp"),
        P(),
        P(),
        P(None, "mp"),
        P(None, "mp"),
        P(None, "mp"),
        P("mp", None),
        P(None, "mp"),
        P(None, "mp"),
        P("mp", None),
    )
    out_specs = (
        P(("dp", "mp"), None),
        P(("dp", "mp"), None),
        P(),
        P(),
        P(None, "mp"),
        P(None, "mp"),
        P(None, "mp"),
        P("mp", None),
        P(None, "mp"),
        P(None, "mp"),
        P("mp", None),
    )
    return jax.shard_map(local, mesh=mesh, in_specs=in_specs, out_specs=out_specs, check_vma=False)
```

profile of v0, /device:TPU:0, one launch (start us, length us, event | category | flops | bytes accessed | tf_op | source)
XLA Modules:
  0.0 1727.3 jit_solution(16116755077285871703)
XLA Ops:
  12.9 5.2 all-to-all-start
  18.0 4.6 scatter_custom_fusion.1
  22.6 4.3 all-to-all-start.1
  28.3 17.6 %all-to-all-done.1 = bf16[8,48,1792]{2,1,0:T(8,128)(2,1)S(1)} async-done(((bf16[8,48,1792]{2,1,0:T(8,128)(2,1)}), bf16[8,48,1792]{2,1,0:T(8,128)(2,1)S(1)}, u32[]{:S(2)}, u32[]{:S(2)}) %all-to-all-start.1) | async-done | bytes 1376288 | tf_op jit(solution)/shard_map/all_to_all | solution.py:183
  45.9 3.8 scatter_custom_fusion.2
  50.2 101.4 %all-gather.4.cloned.1.call-done = bf16[1536,1792]{1,0:T(8,128)(2,1)} async-done(((bf16[384,1792]{1,0:T(8,128)(2,1)}), bf16[1536,1792]{1,0:T(8,128)(2,1)}) %all-gather.4.cloned.1.call-update) | async-done | bytes 5505040 | tf_op jit(solution)/shard_map/all_gather | solution.py:213
  151.6 3.8 fusion.55
  157.2 4.0 convolution_convert_fusion.10
  169.8 26.9 %while.30 = (s32[]{:T(128)}, bf16[3,512,4,112]{1,3,2,0:T(8,128)(2,1)}, f32[3,4,512]{2,1,0:T(4,128)S(1)}, s32[3]{0:T(128)S(1)}, bf16[1600,4,112]{0,2,1:T(8,128)(2...) while((s32[]{:T(128)}, ...), condition=%wide.region_12.13_spmd, body=%wide.region_9.12_spmd.sunk | while | flops 545521280 | bytes 17490852 | solution.py:81
  200.4 3.9 reshape.374
  204.2 7.9 fusion.83
  212.2 4.6 scatter_custom_fusion.3
  216.8 23.1 %all_to_all.60 = bf16[8,48,1792]{2,1,0:T(8,128)(2,1)} all-to-all(bf16[8,48,1792]{2,1,0:T(8,128)(2,1)} %bitcast.130), channel_id=1, replica_groups=mesh['dp'=8,'mp'=4] {'dp'}, dimensions={0} | all-to-all | bytes 2752512 | tf_op jit(solution)/shard_map/all_to_all | solution.py:190
  240.0 4.6 scatter_custom_fusion.4
  244.6 341.4 %all-reduce.9.cloned.1.call-done = f32[1536,1792]{1,0:T(8,128)} async-done(((f32[1536,1792]{1,0:T(8,128)}), f32[1536,1792]{1,0:T(8,128)}) %all-reduce.9.cloned.1.call-update) | async-done | bytes 11010064 | tf_op jit(solution)/shard_map/psum | solution.py:227
  586.1 11.9 multiply_reduce_fusion.1
  597.9 5.1 multiply_convert_fusion.1
  603.1 11.5 fusion.84
  614.6 7.7 fusion.85
  622.3 66.7 %all-gather.6.cloned.1.call-done = bf16[1536,1792]{1,0:T(8,128)(2,1)} async-done(((bf16[384,1792]{1,0:T(8,128)(2,1)}), bf16[1536,1792]{1,0:T(8,128)(2,1)}) %all-gather.6.cloned.1.call-update) | async-done | bytes 5505040 | tf_op jit(solution)/shard_map/all_gather | solution.py:214
  689.0 16.0 multiply_convert_fusion.2
  705.1 8.5 fusion.86
  713.6 11.2 convolution_add_fusion
  726.9 182.8 %reduce-scatter.6.cloned.1.call-done = f32[384,1792]{1,0:T(8,128)} async-done(((f32[1536,1792]{1,0:T(8,128)}), f32[384,1792]{1,0:T(8,128)}) %reduce-scatter.6.cloned.1.call-update) | async-done | bytes 2752528 | tf_op jit(solution)/shard_map/reduce_scatter | solution.py:253
  909.8 4.1 multiply_reduce_fusion.2
  914.4 3.7 fusion.82
  918.2 103.5 %all-gather.8.cloned.1.call-done = bf16[1536,1792]{1,0:T(8,128)(2,1)} async-done(((bf16[384,1792]{1,0:T(8,128)(2,1)}), bf16[1536,1792]{1,0:T(8,128)(2,1)}) %all-gather.8.cloned.1.call-update) | async-done | bytes 5505040 | tf_op jit(solution)/shard_map/all_gather | solution.py:262
  1021.8 7.1 convolution_convert_fusion.8
  1032.5 127.1 %while.31 = (s32[]{:T(128)}, f32[1600,4,112]{0,2,1:T(8,128)}, f32[1600,4,112]{0,2,1:T(8,128)}, bf16[3,512,4,112]{1,3,2,0:T(8,128)(2,1)}, s32[3]{0:T(128)S(1)}, /...) while((s32[]{:T(128)}, f32[1600,4,112]{0,2,1:T(8,128)}, ...), condition=%wide.region_24.25_spmd, body=%wide.region_22.24_spmd.sunk | while | flops 1342557824 | bytes 73204776 | solution.py:143
  1033.8 4.5 fusion.164
  1039.1 4.7 multiply_reduce_fusion.6
  1049.1 9.8 dynamic_update_slice.44
  1058.9 4.4 fusion.167
  1063.3 9.8 dynamic_update_slice.45
  1077.4 4.5 fusion.164
  1082.8 4.7 multiply_reduce_fusion.6
  1092.8 9.7 dynamic_update_slice.44
  1102.5 4.4 fusion.167
  1106.8 9.7 dynamic_update_slice.45
  1120.8 4.5 fusion.164
  1126.2 4.6 multiply_reduce_fusion.6
  1136.0 8.1 dynamic_update_slice.44
  1144.2 4.3 fusion.167
  1148.5 8.1 dynamic_update_slice.45
  1165.0 4.9 fusion.87
  1172.4 5.7 fusion.88
  1180.5 7.5 add_convert_fusion
  1188.0 10.1 convolution_convert_fusion
  1198.2 10.7 convolution_convert_fusion.1
  1209.0 10.3 convolution_convert_fusion.3
  1219.3 7.4 convolution_convert_fusion.2
  1230.5 3.9 convolution_convert_fusion.4
  1234.4 3.9 convolution_convert_fusion.7
  1238.3 3.9 convolution_convert_fusion.6
  1243.9 40.6 %reduce-scatter.8.cloned.1.call-done = bf16[384,1792]{1,0:T(8,128)(2,1)} async-done(((bf16[1536,1792]{1,0:T(8,128)(2,1)}), bf16[384,1792]{1,0:T(8,128)(2,1)}) %reduce-scatter.8.cloned.1.call-update) | async-done | bytes 1376272 | tf_op jit(solution)/shard_map/reduce_scatter | solution.py:279
  1286.8 99.1 %reduce-scatter.4.cloned.1.call-done = bf16[384,1792]{1,0:T(8,128)(2,1)} async-done(((bf16[1536,1792]{1,0:T(8,128)(2,1)}), bf16[384,1792]{1,0:T(8,128)(2,1)}) %reduce-scatter.4.cloned.1.call-update) | async-done | bytes 1376272 | tf_op jit(solution)/shard_map/reduce_scatter | solution.py:237
  1385.9 5.2 fusion.63
  1400.7 30.8 %all-to-all-done.2 = bf16[8,48,1792]{2,1,0:T(8,128)(2,1)S(1)} async-done(((bf16[8,48,1792]{2,1,0:T(8,128)(2,1)}), bf16[8,48,1792]{2,1,0:T(8,128)(2,1)S(1)}, u32[]{:S(2)}, u32[]{:S(2)}) %all-to-all-start.2) | async-done | bytes 1376288 | tf_op jit(solution)/shard_map/all_to_all | solution.py:302
  1431.5 4.6 all-to-all-start.4
  1436.1 213.3 %all-reduce.11.cloned.1.call-done = (bf16[1792,448]{0,1:T(8,128)(2,1)}, bf16[1792,448]{0,1:T(8,128)(2,1)}, bf16[1792,448]{0,1:T(8,128)(2,1)}, bf16[448,1792]{1,0...) async-done(((bf16[1792,448]{0,1:T(8,128)(2,1)}, bf16[1792,448]{0,1:T(8,128)(2,1)}, bf16[1792,448]{0,1:T(8,128)(2,1)}, ...) | async-done | bytes 17432592 | tf_op jit(solution)/shard_map/psum | solution.py:293
  1659.9 3.9 convert_element_type.185
  1663.9 3.9 convert_element_type.187
  1671.4 39.4 %all-reduce.4 = (f32[1792]{0:T(1024)}, f32[1792]{0:T(1024)}) all-reduce(f32[1792]{0:T(1024)S(1)} %get-tuple-element.307, f32[1792]{0:T(1024)S(1)} %copy-done.27), channel_id=1, replica_groups=mesh['dp'=8,'mp'=4] {'dp','mp'}, use_global_device_ids=true, to_apply=%region_28.29 | all-reduce | flops 3584 | bytes 28672 | tf_op jit(solution)/shard_map/psum | solution.py:291
  1713.8 6.2 gather_fusion.3
  (265 shorter events, 126.7 us)
Async XLA Ops:
  7.2 197.1 %copy-start = (bf16[448,1792]{1,0:T(8,128)(2,1)S(1)}, bf16[448,1792]{1,0:T(8,128)(2,1)}, u32[]{:S(2)}) copy-start(bf16[448,1792]{1,0:T(8,128)(2,1)} %param.28) | copy-start | bytes 4816900
  9.3 203.0 %copy-start.30 = (s32[384]{0:T(512)}, s32[384]{0:T(512)S(1)}, u32[]{:S(2)}) copy-start(s32[384]{0:T(512)S(1)} %compare_select_fusion.1) | copy-start | bytes 4612
  12.9 9.8 all-to-all-start
  22.6 27.1 %copy-start.41 = (s32[1,3]{1,0:T(1,128)S(1)}, s32[1,3]{1,0:T(1,128)}, u32[]{:S(2)}) copy-start(s32[1,3]{1,0:T(1,128)} %param.21) | copy-start | bytes 40
  22.6 27.3 %copy-start.34 = (s32[1536]{0:T(1024)S(1)}, s32[1536]{0:T(1024)}, u32[]{:S(2)}) copy-start(s32[1536]{0:T(1024)} %param.22) | copy-start | bytes 18436
  22.6 23.2 %all-to-all-start.1 = ((bf16[8,48,1792]{2,1,0:T(8,128)(2,1)}), bf16[8,48,1792]{2,1,0:T(8,128)(2,1)S(1)}, u32[]{:S(2)}, u32[]{:S(2)}) async-start(bf16[8,48,1792]{2,1,0:T(8,128)(2,1)} %bitcast.14), calls=%async_computation.1 | async-start | bytes 2752512 | tf_op jit(solution)/shard_map/all_to_all | solution.py:183
  26.9 124.7 %all-gather.4.cloned.1.call-start = ((), (), s32[]{:S(2)}) async-start(), calls=%async_computation.8 | async-start | bytes 6881280 | tf_op jit(solution)/shard_map/all_gather | solution.py:213
  28.3 211.7 %copy-start.32 = (s32[384]{0:T(512)}, s32[384]{0:T(512)S(1)}, u32[]{:S(2)}) copy-start(s32[384]{0:T(512)S(1)} %fusion.79) | copy-start | bytes 4612
  49.7 536.4 %all-reduce.9.cloned.1.call-start = ((), (), s32[]{:S(2)}) async-start(), calls=%async_computation.9 | async-start | bytes 22020096 | tf_op jit(solution)/shard_map/psum | solution.py:227
  50.2 105.3 %copy-start.23 = (f32[1792]{0:T(1024)S(1)}, f32[1792]{0:T(1024)}, u32[]{:S(2)}) copy-start(f32[1792]{0:T(1024)} %param.23) | copy-start | bytes 21508
  151.6 4.2 copy-start.3
  157.2 7.3 copy-start.8
  157.2 4.0 copy-start.39
  212.2 476.8 %all-gather.6.cloned.1.call-start = ((), (), s32[]{:S(2)}) async-start(), calls=%async_computation.11 | async-start | bytes 6881280 | tf_op jit(solution)/shard_map/all_gather | solution.py:214
  244.6 353.4 %copy-start.21 = (f32[1792]{0:T(1024)S(1)}, f32[1792]{0:T(1024)}, u32[]{:S(2)}) copy-start(f32[1792]{0:T(1024)} %param.24) | copy-start | bytes 21508
  244.6 665.2 %reduce-scatter.6.cloned.1.call-start = ((), (), s32[]{:S(2)}) async-start(), calls=%async_computation.12 | async-start | bytes 13762560 | tf_op jit(solution)/shard_map/reduce_scatter | solution.py:253
  603.1 11.6 copy-start.7
  603.1 11.6 copy-start.36
  689.0 16.0 copy-start.35
  705.0 8.6 copy-start.44
  705.0 8.6 copy-start.42
  705.0 8.6 copy-start.37
  724.8 297.0 %all-gather.8.cloned.1.call-start = ((), (), s32[]{:S(2)}) async-start(), calls=%async_computation.13 | async-start | bytes 6881280 | tf_op jit(solution)/shard_map/all_gather | solution.py:262
  726.9 186.9 %copy-start.25 = (f32[384]{0:T(512)}, f32[384]{0:T(512)S(1)}, u32[]{:S(2)}) copy-start(f32[384]{0:T(512)S(1)} %add_rsqrt_fusion.3) | copy-start | bytes 4612
  909.7 4.7 copy-start.5
  909.7 4.7 copy-start.6
  918.2 366.3 %reduce-scatter.8.cloned.1.call-start = ((), (), s32[]{:S(2)}) async-start(), calls=%async_computation.14 | async-start | bytes 6881280 | tf_op jit(solution)/shard_map/reduce_scatter | solution.py:279
  1039.1 4.7 slice-start
  1039.1 4.7 slice-start.1
  1082.8 4.7 slice-start
  1082.8 4.7 slice-start.1
  1126.2 4.7 slice-start
  1126.2 4.6 slice-start.1
  1169.9 2.4 copy-start.40
  1172.4 5.7 copy-start.19
  1178.1 2.4 copy-start.16
  1188.0 197.9 %reduce-scatter.4.cloned.1.call-start = ((), (), s32[]{:S(2)}) async-start(), calls=%async_computation.10 | async-start | bytes 6881280 | tf_op jit(solution)/shard_map/reduce_scatter | solution.py:237
  1198.1 451.2 %all-reduce.11.cloned.1.call-start = ((), (), s32[]{:S(2)}) async-start(), calls=%async_computation.15 | async-start | bytes 34865152 | tf_op jit(solution)/shard_map/psum | solution.py:293
  1198.2 10.8 copy-start.45
  1198.2 21.1 %slice-start.2 = ((s8[5505024]{0:T(1024)(128)(4,1)}), s8[4194304]{0:T(1024)(128)(4,1)S(1)}, s32[]{:S(2)}) async-start(s8[5505024]{0:T(1024)(128)(4,1)} %bitcast.124), calls=%async_computation.18 | async-start | bytes 8388608
  1208.9 10.3 slice-start.3
  1208.9 10.3 copy-start.43
  1208.9 17.8 %slice-start.4 = ((s8[5505024]{0:T(1024)(128)(4,1)}), s8[4194304]{0:T(1024)(128)(4,1)S(1)}, s32[]{:S(2)}) async-start(s8[5505024]{0:T(1024)(128)(4,1)} %bitcast.128), calls=%async_computation.20 | async-start | bytes 8388608
  1219.3 7.4 slice-start.5
  1219.3 7.4 copy-start.20
  1226.7 11.6 slice-start.6
  1230.5 3.9 copy-start.18
  1230.5 7.8 slice-start.7
  1234.4 3.9 copy-start.17
  1242.2 42.3 %copy-start.24 = (f32[1792]{0:T(1024)S(1)}, f32[1792]{0:T(1024)}, u32[]{:S(2)}) copy-start(f32[1792]{0:T(1024)} %param.23) | copy-start | bytes 21508
  1242.8 143.1 %copy-start.22 = (f32[1792]{0:T(1024)S(1)}, f32[1792]{0:T(1024)}, u32[]{:S(2)}) copy-start(f32[1792]{0:T(1024)} %param.24) | copy-start | bytes 21508
  1242.8 143.1 %copy-start.26 = (f32[384]{0:T(512)S(1)}, f32[384]{0:T(512)}, u32[]{:S(2)}) copy-start(f32[384]{0:T(512)} %copy-done.25) | copy-start | bytes 4612
  1242.8 143.1 %copy-start.29 = (f32[384]{0:T(512)S(1)}, f32[384]{0:T(512)}, u32[]{:S(2)}) copy-start(f32[384]{0:T(512)} %copy-done.28) | copy-start | bytes 4612
  1394.1 37.5 %all-to-all-start.2 = ((bf16[8,48,1792]{2,1,0:T(8,128)(2,1)}), bf16[8,48,1792]{2,1,0:T(8,128)(2,1)S(1)}, u32[]{:S(2)}, u32[]{:S(2)}) async-start(bf16[8,48,1792]{2,1,0:T(8,128)(2,1)} %bitcast.127), calls=%async_computation.3 | async-start | bytes 2752512 | tf_op jit(solution)/shard_map/all_to_all | solution.py:302
  1400.7 35.4 %copy-start.31 = (s32[384]{0:T(512)S(1)}, s32[384]{0:T(512)}, u32[]{:S(2)}) copy-start(s32[384]{0:T(512)} %copy-done.30) | copy-start | bytes 4612
  1431.5 282.3 %all-to-all-start.4 = ((bf16[8,48,1792]{2,1,0:T(8,128)(2,1)}), bf16[8,48,1792]{2,1,0:T(8,128)(2,1)}, u32[]{:S(2)}, u32[]{:S(2)}) async-start(bf16[8,48,1792]{2,1,0:T(8,128)(2,1)} %bitcast.126), calls=%async_computation.7 | async-start | bytes 2752512 | tf_op jit(solution)/shard_map/all_to_all | solution.py:309
  1649.4 3.4 copy-start.14
  1652.8 2.0 copy-start.13
  1654.7 2.0 copy-start.12
  1656.7 3.2 copy-start.11
  1659.9 3.9 copy-start.10
  1663.9 3.9 copy-start.9
  1667.8 3.6 copy-start.27
  1713.8 6.2 copy-start.1
  (8 other events, 9.9 us)
Sparse Core Ops, SparseCore 0:
  49.8 101.7 all-gather.3
  212.3 373.7 all-reduce.8
  587.6 101.3 all-gather.5
  724.9 184.7 reduce-scatter.5
  918.3 103.4 all-gather.7
  1188.1 96.3 reduce-scatter.7
  1287.3 98.5 reduce-scatter.3
  1391.7 257.6 all-reduce.10
where the time goes:
time: 1740 us; the launch traced here: 1730 us
  waiting for transfers between devices  1200 us (69%)
  matrix products  226 us (13%)
  local copies, waits for them, and re-layouts  130 us (7%)
  other arithmetic  74.3 us (4%)
  blocking collectives  62.6 us (4%)
  starting transfers between devices  18 us (1%)
    psum x1, waiting for transfers between devices, local(): lax.psum(jnp.dot(mixed_flat, w_out, preferred_element_type=jnp.float32),...  341 us
    psum x1, waiting for transfers between devices, local(): lax.psum(query_sum.astype(jnp.bfloat16), 'dp').astype(jnp.float32)  213 us
    reduce_scatter x1, waiting for transfers between devices, local(): lax.psum_scatter(jnp.einsum('tf,df->td', gate_grad, w_gate, preferred_ele...  183 us
    all_gather x1, waiting for transfers between devices, local(): lax.all_gather(middle_grad.astype(jnp.bfloat16), 'mp', axis=0, tiled=True)  104 us
    all_gather x1, waiting for transfers between devices, local(): lax.all_gather(token_rows, 'mp', axis=0, tiled=True)  101 us
    reduce_scatter x1, waiting for transfers between devices, local(): lax.psum_scatter(jnp.dot(activated, w_down, preferred_element_type=jnp.fl...  99.1 us
    all_gather x1, waiting for transfers between devices, local(): lax.all_gather(grad_rows, 'mp', axis=0, tiled=True)  66.7 us
    reduce_scatter x1, waiting for transfers between devices, local(): lax.psum_scatter((jnp.einsum('tc,dc->td', query_grad, w_query, preferred_...  40.6 us
  transfers between devices with their start and end apart: 12, of which 10 were waited for; matrix products, arithmetic and copies ran while one was open for 8% of the time, Pallas kernels for 0%

commit v1 on v0

--- a/solution.py
+++ b/solution.py
@@ -288,7 +288,12 @@
     ).astype(jnp.float32)
     norm_part_one, gain_one_grad = norm_back(hidden_one_grad, normed_one, inverse_one, norm1_gain)
     input_grad = middle_grad + norm_part_one
-    gain_one_sum, gain_two_sum = lax.psum((gain_one_grad, gain_two_grad), ("dp", "mp"))
+
+    def _keep_up_vectors(vals):
+        current_value = lax.psum(vals, axis_name="mp")
+        return lax.psum(current_value, axis_name="dp")
+
+    gain_one_sum, gain_two_sum = _keep_up_vectors((gain_one_grad, gain_two_grad))
     weight_sums = (
         lax.psum(query_sum.astype(jnp.bfloat16), "dp").astype(jnp.float32),
         lax.psum(key_sum.astype(jnp.bfloat16), "dp").astype(jnp.float32),

time: 1740 us -> 1740 us (level)
    psum x1 -> x2, blocking collectives: 39.4 us -> 41.6 us  [the longest x1 22.9 us: _keep_up_vectors(): return lax.psum(current_value, axis_name='dp')]
where the time goes in v1:
time: 1740 us; the launch traced here: 1730 us
  waiting for transfers between devices  1200 us (69%)
  matrix products  226 us (13%)
  local copies, waits for them, and re-layouts  129 us (7%)
  other arithmetic  74.3 us (4%)
  blocking collectives  64.8 us (4%)
  starting transfers between devices  18 us (1%)
    psum x1, waiting for transfers between devices, local(): lax.psum(jnp.dot(mixed_flat, w_out, preferred_element_type=jnp.float32),...  341 us
    psum x1, waiting for transfers between devices, local(): lax.psum(query_sum.astype(jnp.bfloat16), 'dp').astype(jnp.float32)  213 us
    reduce_scatter x1, waiting for transfers between devices, local(): lax.psum_scatter(jnp.einsum('tf,df->td', gate_grad, w_gate, preferred_ele...  183 us
    all_gather x1, waiting for transfers between devices, local(): lax.all_gather(middle_grad.astype(jnp.bfloat16), 'mp', axis=0, tiled=True)  104 us
    all_gather x1, waiting for transfers between devices, local(): lax.all_gather(token_rows, 'mp', axis=0, tiled=True)  101 us
    reduce_scatter x1, waiting for transfers between devices, local(): lax.psum_scatter(jnp.dot(activated, w_down, preferred_element_type=jnp.fl...  99.1 us
    all_gather x1, waiting for transfers between devices, local(): lax.all_gather(grad_rows, 'mp', axis=0, tiled=True)  66.7 us
    reduce_scatter x1, waiting for transfers between devices, local(): lax.psum_scatter((jnp.einsum('tc,dc->td', query_grad, w_query, preferred_...  40.6 us
  transfers between devices with their start and end apart: 12, of which 10 were waited for; matrix products, arithmetic and copies ran while one was open for 8% of the time, Pallas kernels for 0%

profile of v1, /device:TPU:0, one launch (start us, length us, event | category | flops | bytes accessed | tf_op | source)
XLA Modules:
  0.0 1728.4 jit_solution(17893738782248803331)
XLA Ops:
  12.9 5.2 all-to-all-start
  18.0 4.6 scatter_custom_fusion.1
  22.6 4.3 all-to-all-start.1
  28.3 17.6 %all-to-all-done.1 = bf16[8,48,1792]{2,1,0:T(8,128)(2,1)S(1)} async-done(((bf16[8,48,1792]{2,1,0:T(8,128)(2,1)}), bf16[8,48,1792]{2,1,0:T(8,128)(2,1)S(1)}, u32[]{:S(2)}, u32[]{:S(2)}) %all-to-all-start.1) | async-done | bytes 1376288 | tf_op jit(solution)/shard_map/all_to_all | solution.py:183
  45.9 3.8 scatter_custom_fusion.2
  50.2 101.4 %all-gather.4.cloned.1.call-done = bf16[1536,1792]{1,0:T(8,128)(2,1)} async-done(((bf16[384,1792]{1,0:T(8,128)(2,1)}), bf16[1536,1792]{1,0:T(8,128)(2,1)}) %all-gather.4.cloned.1.call-update) | async-done | bytes 5505040 | tf_op jit(solution)/shard_map/all_gather | solution.py:213
  151.6 3.8 fusion.55
  157.2 4.0 convolution_convert_fusion.10
  169.8 26.9 %while.30 = (s32[]{:T(128)}, bf16[3,512,4,112]{1,3,2,0:T(8,128)(2,1)}, f32[3,4,512]{2,1,0:T(4,128)S(1)}, s32[3]{0:T(128)S(1)}, bf16[1600,4,112]{0,2,1:T(8,128)(2...) while((s32[]{:T(128)}, ...), condition=%wide.region_12.13_spmd, body=%wide.region_9.12_spmd.sunk | while | flops 545521280 | bytes 17490852 | solution.py:81
  200.4 3.9 reshape.374
  204.3 7.9 fusion.83
  212.3 4.6 scatter_custom_fusion.3
  216.9 23.1 %all_to_all.60 = bf16[8,48,1792]{2,1,0:T(8,128)(2,1)} all-to-all(bf16[8,48,1792]{2,1,0:T(8,128)(2,1)} %bitcast.130), channel_id=1, replica_groups=mesh['dp'=8,'mp'=4] {'dp'}, dimensions={0} | all-to-all | bytes 2752512 | tf_op jit(solution)/shard_map/all_to_all | solution.py:190
  240.0 4.6 scatter_custom_fusion.4
  244.7 341.4 %all-reduce.10.cloned.1.call-done = f32[1536,1792]{1,0:T(8,128)} async-done(((f32[1536,1792]{1,0:T(8,128)}), f32[1536,1792]{1,0:T(8,128)}) %all-reduce.10.cloned.1.call-update) | async-done | bytes 11010064 | tf_op jit(solution)/shard_map/psum | solution.py:227
  586.1 11.9 multiply_reduce_fusion.1
  598.0 5.1 multiply_convert_fusion.1
  603.1 11.6 fusion.84
  614.7 7.7 fusion.85
  622.4 66.7 %all-gather.6.cloned.1.call-done = bf16[1536,1792]{1,0:T(8,128)(2,1)} async-done(((bf16[384,1792]{1,0:T(8,128)(2,1)}), bf16[1536,1792]{1,0:T(8,128)(2,1)}) %all-gather.6.cloned.1.call-update) | async-done | bytes 5505040 | tf_op jit(solution)/shard_map/all_gather | solution.py:214
  689.1 16.0 multiply_convert_fusion.2
  705.1 8.5 fusion.86
  713.6 11.2 convolution_add_fusion
  726.9 182.8 %reduce-scatter.6.cloned.1.call-done = f32[384,1792]{1,0:T(8,128)} async-done(((f32[1536,1792]{1,0:T(8,128)}), f32[384,1792]{1,0:T(8,128)}) %reduce-scatter.6.cloned.1.call-update) | async-done | bytes 2752528 | tf_op jit(solution)/shard_map/reduce_scatter | solution.py:253
  909.8 4.1 multiply_reduce_fusion.2
  918.3 103.5 %all-gather.8.cloned.1.call-done = bf16[1536,1792]{1,0:T(8,128)(2,1)} async-done(((bf16[384,1792]{1,0:T(8,128)(2,1)}), bf16[1536,1792]{1,0:T(8,128)(2,1)}) %all-gather.8.cloned.1.call-update) | async-done | bytes 5505040 | tf_op jit(solution)/shard_map/all_gather | solution.py:262
  1021.8 7.1 convolution_convert_fusion.8
  1032.5 127.1 %while.31 = (s32[]{:T(128)}, f32[1600,4,112]{0,2,1:T(8,128)}, f32[1600,4,112]{0,2,1:T(8,128)}, bf16[3,512,4,112]{1,3,2,0:T(8,128)(2,1)}, s32[3]{0:T(128)S(1)}, /...) while((s32[]{:T(128)}, f32[1600,4,112]{0,2,1:T(8,128)}, ...), condition=%wide.region_24.25_spmd, body=%wide.region_22.24_spmd.sunk | while | flops 1342557824 | bytes 73204776 | solution.py:143
  1033.8 4.5 fusion.164
  1039.2 4.7 multiply_reduce_fusion.6
  1049.1 9.8 dynamic_update_slice.44
  1058.9 4.4 fusion.167
  1063.3 9.8 dynamic_update_slice.45
  1077.5 4.5 fusion.164
  1082.8 4.7 multiply_reduce_fusion.6
  1092.8 9.7 dynamic_update_slice.44
  1102.5 4.4 fusion.167
  1106.8 9.7 dynamic_update_slice.45
  1120.8 4.5 fusion.164
  1126.2 4.6 multiply_reduce_fusion.6
  1136.0 8.1 dynamic_update_slice.44
  1144.2 4.3 fusion.167
  1148.4 8.1 dynamic_update_slice.45
  1163.8 5.0 fusion.87
  1171.2 5.7 fusion.88
  1179.3 7.4 add_convert_fusion
  1186.9 10.1 convolution_convert_fusion
  1197.0 10.7 convolution_convert_fusion.1
  1207.8 10.3 convolution_convert_fusion.3
  1218.2 7.4 convolution_convert_fusion.2
  1229.4 3.9 convolution_convert_fusion.4
  1233.3 3.9 convolution_convert_fusion.7
  1237.2 3.9 convolution_convert_fusion.6
  1242.7 40.6 %reduce-scatter.8.cloned.1.call-done = bf16[384,1792]{1,0:T(8,128)(2,1)} async-done(((bf16[1536,1792]{1,0:T(8,128)(2,1)}), bf16[384,1792]{1,0:T(8,128)(2,1)}) %reduce-scatter.8.cloned.1.call-update) | async-done | bytes 1376272 | tf_op jit(solution)/shard_map/reduce_scatter | solution.py:279
  1285.6 99.1 %reduce-scatter.4.cloned.1.call-done = bf16[384,1792]{1,0:T(8,128)(2,1)} async-done(((bf16[1536,1792]{1,0:T(8,128)(2,1)}), bf16[384,1792]{1,0:T(8,128)(2,1)}) %reduce-scatter.4.cloned.1.call-update) | async-done | bytes 1376272 | tf_op jit(solution)/shard_map/reduce_scatter | solution.py:237
  1384.8 5.2 fusion.63
  1399.6 30.8 %all-to-all-done.2 = bf16[8,48,1792]{2,1,0:T(8,128)(2,1)S(1)} async-done(((bf16[8,48,1792]{2,1,0:T(8,128)(2,1)}), bf16[8,48,1792]{2,1,0:T(8,128)(2,1)S(1)}, u32[]{:S(2)}, u32[]{:S(2)}) %all-to-all-start.2) | async-done | bytes 1376288 | tf_op jit(solution)/shard_map/all_to_all | solution.py:307
  1430.4 4.6 all-to-all-start.4
  1435.0 213.3 %all-reduce.12.cloned.1.call-done = (bf16[1792,448]{0,1:T(8,128)(2,1)}, bf16[1792,448]{0,1:T(8,128)(2,1)}, bf16[1792,448]{0,1:T(8,128)(2,1)}, bf16[448,1792]{1,0...) async-done(((bf16[1792,448]{0,1:T(8,128)(2,1)}, bf16[1792,448]{0,1:T(8,128)(2,1)}, bf16[1792,448]{0,1:T(8,128)(2,1)}, ...) | async-done | bytes 17432592 | tf_op jit(solution)/shard_map/psum | solution.py:298
  1658.8 3.9 convert_element_type.185
  1662.7 3.9 convert_element_type.187
  1670.2 18.7 %all-reduce.5 = (f32[1792]{0:T(1024)S(1)}, f32[1792]{0:T(1024)S(1)}) all-reduce(f32[1792]{0:T(1024)S(1)} %get-tuple-element.307, f32[1792]{0:T(1024)S(1)} %copy-done.28), channel_id=1, replica_groups=mesh['dp'=8,'mp'=4] {'mp'}, use_global_device_ids=true, to_apply=%region_28.29 | all-reduce | flops 3584 | bytes 28672 | tf_op jit(solution)/shard_map/psum | solution.py:293
  1689.0 22.9 %all-reduce.4 = (f32[1792]{0:T(1024)}, f32[1792]{0:T(1024)}) all-reduce(f32[1792]{0:T(1024)S(1)} %get-tuple-element.357, f32[1792]{0:T(1024)S(1)} %get-tuple-element.358), channel_id=1, replica_groups=mesh['dp'=8,'mp'=4] {'dp'}, use_global_device_ids=true, to_apply=%region_29.30 | all-reduce | flops 3584 | bytes 28672 | tf_op jit(solution)/shard_map/psum | solution.py:294
  1714.8 6.2 gather_fusion.3
  (268 shorter events, 129.2 us)
Async XLA Ops:
  7.2 197.1 %copy-start = (bf16[448,1792]{1,0:T(8,128)(2,1)S(1)}, bf16[448,1792]{1,0:T(8,128)(2,1)}, u32[]{:S(2)}) copy-start(bf16[448,1792]{1,0:T(8,128)(2,1)} %param.28) | copy-start | bytes 4816900
  9.3 203.0 %copy-start.31 = (s32[384]{0:T(512)}, s32[384]{0:T(512)S(1)}, u32[]{:S(2)}) copy-start(s32[384]{0:T(512)S(1)} %compare_select_fusion.1) | copy-start | bytes 4612
  12.9 9.8 all-to-all-start
  22.6 27.1 %copy-start.42 = (s32[1,3]{1,0:T(1,128)S(1)}, s32[1,3]{1,0:T(1,128)}, u32[]{:S(2)}) copy-start(s32[1,3]{1,0:T(1,128)} %param.21) | copy-start | bytes 40
  22.6 27.3 %copy-start.35 = (s32[1536]{0:T(1024)S(1)}, s32[1536]{0:T(1024)}, u32[]{:S(2)}) copy-start(s32[1536]{0:T(1024)} %param.22) | copy-start | bytes 18436
  22.6 23.2 %all-to-all-start.1 = ((bf16[8,48,1792]{2,1,0:T(8,128)(2,1)}), bf16[8,48,1792]{2,1,0:T(8,128)(2,1)S(1)}, u32[]{:S(2)}, u32[]{:S(2)}) async-start(bf16[8,48,1792]{2,1,0:T(8,128)(2,1)} %bitcast.14), calls=%async_computation.1 | async-start | bytes 2752512 | tf_op jit(solution)/shard_map/all_to_all | solution.py:183
  26.9 124.7 %all-gather.4.cloned.1.call-start = ((), (), s32[]{:S(2)}) async-start(), calls=%async_computation.8 | async-start | bytes 6881280 | tf_op jit(solution)/shard_map/all_gather | solution.py:213
  28.3 211.7 %copy-start.33 = (s32[384]{0:T(512)}, s32[384]{0:T(512)S(1)}, u32[]{:S(2)}) copy-start(s32[384]{0:T(512)S(1)} %fusion.79) | copy-start | bytes 4612
  49.7 536.4 %all-reduce.10.cloned.1.call-start = ((), (), s32[]{:S(2)}) async-start(), calls=%async_computation.9 | async-start | bytes 22020096 | tf_op jit(solution)/shard_map/psum | solution.py:227
  50.2 105.3 %copy-start.24 = (f32[1792]{0:T(1024)S(1)}, f32[1792]{0:T(1024)}, u32[]{:S(2)}) copy-start(f32[1792]{0:T(1024)} %param.23) | copy-start | bytes 21508
  151.6 4.2 copy-start.3
  157.2 7.4 copy-start.8
  157.2 4.0 copy-start.40
  212.2 476.8 %all-gather.6.cloned.1.call-start = ((), (), s32[]{:S(2)}) async-start(), calls=%async_computation.11 | async-start | bytes 6881280 | tf_op jit(solution)/shard_map/all_gather | solution.py:214
  244.6 353.4 %copy-start.22 = (f32[1792]{0:T(1024)S(1)}, f32[1792]{0:T(1024)}, u32[]{:S(2)}) copy-start(f32[1792]{0:T(1024)} %param.24) | copy-start | bytes 21508
  244.6 665.2 %reduce-scatter.6.cloned.1.call-start = ((), (), s32[]{:S(2)}) async-start(), calls=%async_computation.12 | async-start | bytes 13762560 | tf_op jit(solution)/shard_map/reduce_scatter | solution.py:253
  603.1 11.6 copy-start.7
  603.1 11.6 copy-start.37
  689.1 16.0 copy-start.36
  705.1 8.6 copy-start.45
  705.1 8.6 copy-start.43
  705.1 8.6 copy-start.38
  724.8 297.0 %all-gather.8.cloned.1.call-start = ((), (), s32[]{:S(2)}) async-start(), calls=%async_computation.13 | async-start | bytes 6881280 | tf_op jit(solution)/shard_map/all_gather | solution.py:262
  726.9 186.9 %copy-start.26 = (f32[384]{0:T(512)}, f32[384]{0:T(512)S(1)}, u32[]{:S(2)}) copy-start(f32[384]{0:T(512)S(1)} %add_rsqrt_fusion.3) | copy-start | bytes 4612
  909.8 4.7 copy-start.5
  909.8 4.7 copy-start.6
  918.2 365.1 %reduce-scatter.8.cloned.1.call-start = ((), (), s32[]{:S(2)}) async-start(), calls=%async_computation.14 | async-start | bytes 6881280 | tf_op jit(solution)/shard_map/reduce_scatter | solution.py:279
  1039.1 4.7 slice-start
  1039.1 4.7 slice-start.1
  1082.8 4.7 slice-start
  1082.8 4.7 slice-start.1
  1126.2 4.7 slice-start
  1126.2 4.6 slice-start.1
  1163.8 5.0 copy-start.18
  1168.8 2.4 copy-start.41
  1171.2 5.7 copy-start.20
  1176.9 2.4 copy-start.16
  1186.8 197.9 %reduce-scatter.4.cloned.1.call-start = ((), (), s32[]{:S(2)}) async-start(), calls=%async_computation.10 | async-start | bytes 6881280 | tf_op jit(solution)/shard_map/reduce_scatter | solution.py:237
  1197.0 451.2 %all-reduce.12.cloned.1.call-start = ((), (), s32[]{:S(2)}) async-start(), calls=%async_computation.15 | async-start | bytes 34865152 | tf_op jit(solution)/shard_map/psum | solution.py:298
  1197.0 10.8 copy-start.46
  1197.0 21.1 %slice-start.2 = ((s8[5505024]{0:T(1024)(128)(4,1)}), s8[4194304]{0:T(1024)(128)(4,1)S(1)}, s32[]{:S(2)}) async-start(s8[5505024]{0:T(1024)(128)(4,1)} %bitcast.124), calls=%async_computation.18 | async-start | bytes 8388608
  1207.8 10.3 slice-start.3
  1207.8 10.3 copy-start.44
  1207.8 17.8 %slice-start.4 = ((s8[5505024]{0:T(1024)(128)(4,1)}), s8[4194304]{0:T(1024)(128)(4,1)S(1)}, s32[]{:S(2)}) async-start(s8[5505024]{0:T(1024)(128)(4,1)} %bitcast.128), calls=%async_computation.20 | async-start | bytes 8388608
  1218.1 7.5 slice-start.5
  1218.1 7.4 copy-start.21
  1225.6 11.6 slice-start.6
  1229.3 3.9 copy-start.19
  1229.3 7.8 slice-start.7
  1233.3 3.9 copy-start.17
  1241.0 42.3 %copy-start.25 = (f32[1792]{0:T(1024)S(1)}, f32[1792]{0:T(1024)}, u32[]{:S(2)}) copy-start(f32[1792]{0:T(1024)} %param.23) | copy-start | bytes 21508
  1241.7 143.1 %copy-start.23 = (f32[1792]{0:T(1024)S(1)}, f32[1792]{0:T(1024)}, u32[]{:S(2)}) copy-start(f32[1792]{0:T(1024)} %param.24) | copy-start | bytes 21508
  1241.7 143.1 %copy-start.27 = (f32[384]{0:T(512)S(1)}, f32[384]{0:T(512)}, u32[]{:S(2)}) copy-start(f32[384]{0:T(512)} %copy-done.26) | copy-start | bytes 4612
  1241.7 143.1 %copy-start.30 = (f32[384]{0:T(512)S(1)}, f32[384]{0:T(512)}, u32[]{:S(2)}) copy-start(f32[384]{0:T(512)} %copy-done.29) | copy-start | bytes 4612
  1392.9 37.5 %all-to-all-start.2 = ((bf16[8,48,1792]{2,1,0:T(8,128)(2,1)}), bf16[8,48,1792]{2,1,0:T(8,128)(2,1)S(1)}, u32[]{:S(2)}, u32[]{:S(2)}) async-start(bf16[8,48,1792]{2,1,0:T(8,128)(2,1)} %bitcast.127), calls=%async_computation.3 | async-start | bytes 2752512 | tf_op jit(solution)/shard_map/all_to_all | solution.py:307
  1399.6 35.4 %copy-start.32 = (s32[384]{0:T(512)S(1)}, s32[384]{0:T(512)}, u32[]{:S(2)}) copy-start(s32[384]{0:T(512)} %copy-done.31) | copy-start | bytes 4612
  1430.4 284.5 %all-to-all-start.4 = ((bf16[8,48,1792]{2,1,0:T(8,128)(2,1)}), bf16[8,48,1792]{2,1,0:T(8,128)(2,1)}, u32[]{:S(2)}, u32[]{:S(2)}) async-start(bf16[8,48,1792]{2,1,0:T(8,128)(2,1)} %bitcast.126), calls=%async_computation.7 | async-start | bytes 2752512 | tf_op jit(solution)/shard_map/all_to_all | solution.py:314
  1648.2 3.4 copy-start.14
  1651.6 2.0 copy-start.13
  1655.6 3.2 copy-start.11
  1658.8 3.9 copy-start.10
  1662.7 3.9 copy-start.9
  1666.6 3.6 copy-start.28
  1714.8 6.2 copy-start.1
  (9 other events, 11.9 us)
Sparse Core Ops, SparseCore 0:
  49.8 101.7 all-gather.3
  212.3 373.7 all-reduce.9
  587.7 101.3 all-gather.5
  724.9 184.7 reduce-scatter.5
  918.3 103.4 all-gather.7
  1186.9 96.3 reduce-scatter.7
  1286.2 98.5 reduce-scatter.3
  1390.5 257.6 all-reduce.11
